TPU v7x, 256 devices: a whole 4x4x8 slice. The times are simulated.
256 devices in a mesh: pair: 128 (over y_lo, z, x, core), trow: 2 (over y_hi).
Axes of the slice: x: 4, y: 4 (y_hi: 2, y_lo: 2; y = y_hi * 2 + y_lo), z: 8, core: 2. Of those that a mesh axis runs over, the one named last changes fastest.
Arguments:
- query_bank: bfloat16 [128, 64, 1024], P('pair'), may hold values from -6 to 6
- ref_owner: int32 [1], replicated, may hold values from 0 to 127
- target_feat: bfloat16 [128, 512, 1024], P('pair', None, 'trow'), may hold values from -60 to 60
- valid_rows: int32 [128], P('pair'), may hold values from 2 to 16, as said below
- w_first: bfloat16 [16, 1, 3, 3, 3, 3], replicated, may hold values from -2 to 2
- b_first: float32 [16], replicated, may hold values from -0.5 to 0.5
- w_middle: bfloat16 [16, 16, 3, 3, 3, 3], replicated, may hold values from -0.25 to 0.25
- b_middle: float32 [16], replicated, may hold values from -0.5 to 0.5
- w_last: bfloat16 [1, 16, 3, 3, 3, 3], replicated, may hold values from -0.25 to 0.25
- b_last: float32 [1], replicated, may hold values from -0.5 to 0.5
Outputs:
- scores: float32 [128, 64, 512], P('pair', None, 'trow')
Inputs may be any that keep to these rules, and one draw needn't show every extreme that they name: ref_owner names the group along pair whose window is the reference. Rows of a target grid at or past valid_rows are padding; some pair fills all 16 rows.
All inputs are finite; a program needn't handle non-finite values.
Results may differ from a plain program's by a relative error of at most 0.007.
Values may be sent and summed in bfloat16 or wider, within the bound.
A program may use at most 64 MiB of HBM per device.

v0:
```python
import math
import jax
import jax.numpy as jnp
from jax import lax
from jax.sharding import PartitionSpec as P

WB = 32
WA = 32
EPS_NORM = 1e-06
EPS_PEAK = 1e-05


def extended(cells, sides, width):
    for axis, dim in sides:
        count = lax.axis_size(axis)
        ends = count - 1
        head = lax.slice_in_dim(cells, 0, width, axis=dim)
        tail = lax.slice_in_dim(cells, cells.shape[dim] - width, cells.shape[dim], axis=dim)
        cells = jnp.concatenate(
            [
                lax.ppermute(tail, axis, [(i, (i + 1) % count) for i in range(ends)]),
                cells,
                lax.ppermute(head, axis, [((i + 1) % count, i) for i in range(ends)]),
            ],
            axis=dim,
        )
    return cells


def broadcast(shard, axis, root):
    mine = lax.axis_index(axis) == root
    return lax.psum(jnp.where(mine, shard, jnp.zeros_like(shard)), axis)


def shift_along(values, offset, axis_dim):
    if offset == 0:
        return values
    length = values.shape[axis_dim]
    zero_shape = list(values.shape)
    zero_shape[axis_dim] = abs(offset)
    zero_block = jnp.zeros(zero_shape, values.dtype)
    if offset > 0:
        return jnp.concatenate(
            [lax.slice_in_dim(values, offset, length, axis=axis_dim), zero_block], axis=axis_dim
        )
    return jnp.concatenate(
        [zero_block, lax.slice_in_dim(values, 0, length + offset, axis=axis_dim)], axis=axis_dim
    )


def block_conv(row_block, weight_matrix, out_channels, block_rows):
    extent = row_block.shape[2]
    column_pos = jnp.arange(extent, dtype=jnp.int32) % WB
    shifted = []
    for col_off in (-1, 0, 1):
        in_range = (column_pos + col_off >= 0) & (column_pos + col_off < WB)
        moved_cols = shift_along(row_block, col_off, 2)
        shifted.append(
            jnp.where(in_range[None, None, :], moved_cols, jnp.zeros((), row_block.dtype))
        )
    layers = []
    for row_off in range(3):
        for col_idx in range(3):
            layers.append(
                lax.slice_in_dim(
                    shifted[col_idx], row_off * WB, (row_off + block_rows) * WB, axis=2
                )
            )
    stacked = jnp.concatenate(layers, axis=0)
    products = jnp.einsum("pk,kab->pab", weight_matrix, stacked, preferred_element_type=jnp.float32)
    positions = row_block.shape[1]
    query_row = jnp.arange(positions, dtype=jnp.int32) // WA
    query_col = jnp.arange(positions, dtype=jnp.int32) % WA
    ref_rows = positions // WA
    accumulated = jnp.zeros((out_channels, positions, block_rows * WB), jnp.float32)
    for row_off in range(3):
        for col_off in range(3):
            start_chan = (row_off * 3 + col_off) * out_channels
            offset_group = products[start_chan : start_chan + out_channels]
            in_range = (query_row + row_off - 1 >= 0) & (query_row + row_off - 1 < ref_rows)
            in_range = in_range & (query_col + col_off - 1 >= 0) & (query_col + col_off - 1 < WA)
            moved_group = shift_along(offset_group, (row_off - 1) * WA + col_off - 1, 1)
            accumulated = accumulated + jnp.where(in_range[None, :, None], moved_group, 0.0)
    return accumulated


def conv_layer(inputs, weight, bias):
    out_channels = weight.shape[0]
    in_channels = weight.shape[1]
    weight_matrix = jnp.transpose(weight, (2, 3, 0, 4, 5, 1)).reshape(
        9 * out_channels, 9 * in_channels
    )
    rows_out = inputs.shape[2] // WB - 2
    block_rows = 1
    for option in (2, 4):
        block_rows = option

    def one_block(block_index):
        row_block = lax.dynamic_slice_in_dim(
            inputs, block_index * (block_rows * WB), (block_rows + 2) * WB, 2
        )
        return block_conv(row_block, weight_matrix, out_channels, block_rows)

    block_outputs = lax.map(one_block, jnp.arange(rows_out // block_rows, dtype=jnp.int32))
    joined = jnp.transpose(block_outputs, (1, 2, 0, 3)).reshape(
        out_channels, inputs.shape[1], rows_out * WB
    )
    return joined + bias[:, None, None]


def unit_rows(features):
    values = features.astype(jnp.float32)
    return (values * lax.rsqrt(jnp.sum(values * values, axis=1, keepdims=True) + EPS_NORM)).astype(
        jnp.bfloat16
    )


def contract(left, right):
    return lax.dot_general(
        left, right, (((1,), (1,)), ((), ())), preferred_element_type=jnp.float32
    )


def score_pair(raw_dot, squares, trow_rank, row_count, cos_scale, weights):
    w_first, b_first, w_middle, b_middle, w_last, b_last = weights
    rows_here = raw_dot.shape[1] // WB
    first_row = trow_rank * rows_here
    global_row = first_row + jnp.arange(raw_dot.shape[1], dtype=jnp.int32) // WB
    is_live = global_row < row_count
    correlation = jnp.where(
        is_live[None, :], cos_scale * raw_dot * lax.rsqrt(squares + EPS_NORM)[None, :], 0.0
    )
    magnitude = jnp.abs(correlation)
    peak_query = jnp.max(magnitude, axis=0)
    peak_target = lax.pmax(jnp.max(magnitude, axis=1), "trow")
    volume = (
        correlation
        * (correlation / (peak_query[None, :] + EPS_PEAK))
        * (correlation / (peak_target[:, None] + EPS_PEAK))
    )
    volume = volume.astype(jnp.bfloat16)[None]
    padded = extended(volume, (("trow", 2),), WB)
    hidden = jnp.maximum(conv_layer(padded, w_first, b_first), 0.0).astype(jnp.bfloat16)
    padded = extended(hidden, (("trow", 2),), WB)
    hidden = jnp.maximum(conv_layer(padded, w_middle, b_middle), 0.0).astype(jnp.bfloat16)
    padded = extended(hidden, (("trow", 2),), WB)
    result = conv_layer(padded, w_last, b_last)[0]
    return jnp.where(is_live[None, :], result, 0.0)


def per_device(
    query_bank,
    ref_owner,
    target_feat,
    valid_rows,
    w_first,
    b_first,
    w_middle,
    b_middle,
    w_last,
    b_last,
):
    query_vec = broadcast(query_bank[0], "pair", ref_owner[0])
    unit_query = unit_rows(query_vec)
    cos_scale = math.sqrt(query_vec.shape[1])
    trow_rank = lax.axis_index("trow")
    weights = (w_first, b_first, w_middle, b_middle, w_last, b_last)
    exchanged = lax.all_to_all(target_feat, "trow", split_axis=1, concat_axis=2, tiled=True)
    local_rows = exchanged[0]
    raw_dot = contract(unit_query, local_rows)
    squares = jnp.sum(jnp.square(local_rows.astype(jnp.float32)), axis=1)
    scores = [score_pair(raw_dot, squares, trow_rank, valid_rows[0], cos_scale, weights)]
    return jnp.stack(scores)


def solution(mesh):
    in_specs = (
        P("pair", None, None),
        P(),
        P("pair", None, "trow"),
        P("pair"),
        P(),
        P(),
        P(),
        P(),
        P(),
        P(),
    )
    out_specs = P("pair", None, "trow")
    return jax.shard_map(
        per_device, mesh=mesh, in_specs=in_specs, out_specs=out_specs, check_vma=False
    )
```

profile of v0, /device:TPU:8, one launch (start us, length us, event | category | flops | bytes accessed | tf_op | source)
XLA Modules:
  0.0 1043.2 jit_solution(17501619991861130497)
XLA Ops:
  7.2 0.7 select_bitcast_fusion
  7.9 1.9 copy.50
  9.7 0.5 broadcast.3951
  10.3 3.8 reduce.1
  14.1 1.1 reshape.509
  15.2 3.6 all-to-all-start
  19.4 938.0 %all-reduce.32.cloned.1.call-done = bf16[64,1024]{1,0:T(8,128)(2,1)} async-done(((bf16[64,1024]{1,0:T(8,128)(2,1)}), bf16[64,1024]{1,0:T(8,128)(2,1)}) %all-reduce.32.cloned.1.call-update) | async-done | bytes 131088 | tf_op jit(solution)/shard_map/psum | solution.py:32
  957.5 1.0 fusion.30
  958.5 0.5 reshape.510
  959.9 6.4 pmax.7
  966.6 4.3 collective-permute-start
  970.9 1.3 collective-permute-start.1
  972.3 5.7 collective-permute-done.1
  978.2 10.4 while.45
  978.2 0.6 dynamic_slice.71
  980.6 0.5 concatenate.223
  981.0 0.8 convolution_bitcast_fusion.6
  982.1 1.2 fusion.97
  983.4 0.6 dynamic_slice.71
  985.7 0.5 concatenate.223
  986.2 0.8 convolution_bitcast_fusion.6
  987.3 1.2 fusion.97
  988.9 1.7 collective-permute-start.2
  990.6 1.5 collective-permute-start.3
  992.5 1.9 collective-permute-done.2
  994.4 5.9 collective-permute-done.3
  1000.3 0.5 pad_maximum_fusion
  1000.9 11.8 %while.46 = (s32[]{:T(128)}, f32[2,16,64,128]{3,1,2,0:T(8,128)S(1)}, s32[2]{0:T(128)S(1)}, bf16[16,64,320]{2,0,1:T(8,128)(2,1)S(1)}, bf16[144,144]{1,0:T(8,128)(...) while((s32[]{:T(128)}, f32[2,16,64,128]{3,1,2,0:T(8,128)S(1)}, s32[2]{0:T(128)S(1)}, ...), condition=%wide.region_9.10_spmd, body=%wide.region_8.9_spmd.sunk | while | flops 342569024 | bytes 24628092 | solution.py:104
  1000.9 0.6 dynamic_slice.73
  1002.2 0.5 constant_dynamic-slice_fusion.9
  1004.5 0.8 convolution_bitcast_fusion.7
  1005.6 1.2 fusion.104
  1006.8 0.6 dynamic_slice.73
  1010.4 0.8 convolution_bitcast_fusion.7
  1011.5 1.2 fusion.104
  1013.1 1.5 collective-permute-start.4
  1014.5 1.3 collective-permute-start.5
  1016.6 1.8 collective-permute-done.4
  1018.4 5.9 collective-permute-done.5
  1024.3 0.5 pad_maximum_fusion.1
  1024.8 10.9 %while.47 = (s32[]{:T(128)}, f32[2,1,64,128]{3,2,1,0:T(8,128)S(1)}, s32[2]{0:T(128)S(1)}, bf16[16,64,320]{2,0,1:T(8,128)(2,1)S(1)}, bf16[9,144]{1,0:T(8,128)(2,1...) while((s32[]{:T(128)}, f32[2,1,64,128]{3,2,1,0:T(8,128)S(1)}, s32[2]{0:T(128)S(1)}, ...), condition=%wide.region_11.12_spmd, body=%wide.region_10.11_spmd.sunk | while | flops 21975112 | bytes 11917275 | solution.py:104
  1024.8 0.6 dynamic_slice.75
  1026.0 0.4 constant_dynamic-slice_fusion.10
  1029.0 1.3 fusion.111
  1030.3 0.6 dynamic_slice.75
  1031.4 0.4 constant_dynamic-slice_fusion.10
  1034.4 1.3 fusion.111
  1035.7 0.6 bitcast_select_fusion
  (182 shorter events, 14.5 us)
Async XLA Ops:
  6.5 950.9 %all-reduce.32.cloned.1.call-start = ((), (), s32[]{:S(2)}) async-start(), calls=%async_computation.1 | async-start | bytes 262144 | tf_op jit(solution)/shard_map/psum | solution.py:32
  15.2 943.3 %all-to-all-start = ((bf16[2,2,65536]{2,1,0:T(2,128)(2,1)}), bf16[2,2,65536]{2,1,0:T(2,128)(2,1)S(1)}, u32[]{:S(2)}, u32[]{:S(2)}) async-start(bf16[2,2,65536]{2,1,0:T(2,128)(2,1)} %reshape.509), calls=%async_computation | async-start | bytes 1048576 | tf_op jit(solution)/shard_map/all_to_all | solution.py:168
  958.5 1.1 copy-start
  959.0 13.1 %copy-start.2 = (bf16[16,1,3,3,3,3]{0,5,4,3,2,1:T(4,128)(2,1)S(1)}, bf16[16,1,3,3,3,3]{0,5,4,3,2,1:T(4,128)(2,1)}, u32[]{:S(2)}) copy-start(bf16[16,1,3,3,3,3]{0,5,4,3,2,1:T(4,128)(2,1)} %param.20) | copy-start | bytes 7780
  966.6 5.7 collective-permute-start
  970.9 7.1 collective-permute-start.1
  978.2 10.4 copy-start.4
  988.6 3.5 copy-start.1
  988.9 5.5 collective-permute-start.2
  990.6 9.8 collective-permute-start.3
  1000.9 11.8 %copy-start.5 = (f32[16]{0:T(128)S(1)}, f32[16]{0:T(128)}, u32[]{:S(2)}) copy-start(f32[16]{0:T(128)} %param.23) | copy-start | bytes 196
  1012.7 3.1 copy-start.3
  1013.1 5.3 collective-permute-start.4
  1014.5 9.8 collective-permute-start.5
Sparse Core Ops, SparseCore 0:
  9.9 947.4 all-reduce.31
where the time goes:
time: 1040 us
  waiting for transfers between devices  959 us (92%)
  local copies, waits for them, and re-layouts  19 us (2%)
  other arithmetic  18.8 us (2%)
  between operations  15.7 us (2%)
  starting transfers between devices  15 us (1%)
    psum x1, waiting for transfers between devices, broadcast(): return lax.psum(jnp.where(mine, shard, jnp.zeros_like(shard)), axis)  938 us
  transfers between devices with their start and end apart: 8, of which 6 were waited for; matrix products, arithmetic and copies ran while one was open for 1% of the time, Pallas kernels for 0%

commit v1 on v0

--- a/solution.py
+++ b/solution.py
@@ -29,7 +29,7 @@
 
 def broadcast(shard, axis, root):
     mine = lax.axis_index(axis) == root
-    return lax.psum(jnp.where(mine, shard, jnp.zeros_like(shard)), axis)
+    return jnp.sum(lax.all_gather(jnp.where(mine, shard, jnp.zeros_like(shard)), axis), axis=0)
 
 
 def shift_along(values, offset, axis_dim):

time: 1040 us -> 335 us (0.32)
  waiting for transfers between devices: 959 us -> 240 us
    psum x1 -> x0, waiting for transfers between devices: 938 us -> none  [broadcast(): return lax.psum(jnp.where(mine, shard, jnp.zeros_like(shard)), axis)]
    all_gather x0 -> x1, waiting for transfers between devices: none -> 209 us  [broadcast(): lax.all_gather(jnp.where(mine, shard, jnp.zeros_like(shard)), axis)]
  transfers between devices with their start and end apart: 8 -> 8, of which waited for: 6 -> 7; matrix products, arithmetic and copies ran while one was open for 1% -> 3% of each run, Pallas kernels for 0% -> 0%
where the time goes in v1:
time: 335 us; the launch traced here: 332 us
  waiting for transfers between devices  240 us (72%)
  other arithmetic  26.8 us (8%)
  local copies, waits for them, and re-layouts  19.2 us (6%)
  between operations  15.7 us (5%)
  starting transfers between devices  15.3 us (5%)
  blocking collectives  6.44 us (2%)
  loops' own time  4.86 us (1%)
  matrix products  4.32 us (1%)
    all_gather x1, waiting for transfers between devices, broadcast(): lax.all_gather(jnp.where(mine, shard, jnp.zeros_like(shard)), axis)  209 us
    ppermute x3, waiting for transfers between devices, extended(): lax.ppermute(head, axis, [((i + 1) % count, i) for i in range(ends)])  17.5 us
    all_to_all x1, waiting for transfers between devices, per_device(): lax.all_to_all(target_feat, 'trow', split_axis=1, concat_axis=2, tiled=True)  9.01 us
    reduce_sum x1, other arithmetic, broadcast(): jnp.sum(lax.all_gather(jnp.where(mine, shard, jnp.zeros_like(shard)), axi...  8.92 us
    ppermute x3, starting transfers between devices, extended(): lax.ppermute(tail, axis, [(i, (i + 1) % count) for i in range(ends)])  7.69 us
  transfers between devices with their start and end apart: 8, of which 7 were waited for; matrix products, arithmetic and copies ran while one was open for 3% of the time, Pallas kernels for 0%

profile of v1, /device:TPU:8, one launch (start us, length us, event | category | flops | bytes accessed | tf_op | source)
XLA Modules:
  0.0 332.1 jit_solution(12050561946764327519)
XLA Ops:
  7.2 0.7 broadcast_select_fusion.12
  7.9 1.9 copy.58
  9.7 0.5 broadcast.3949
  10.3 3.8 %reduce.2 = bf16[512,512]{1,0:T(8,128)(2,1)S(1)} reduce(bf16[512,1,512]{2,1,0:T(2,128)(2,1)S(1)} %bitcast.113, bf16[]{:T(256)} %broadcast.3949), dimensions={1}, to_apply=%bitcast.76.reduce_sub_computation | reduce | bytes 1048578
  14.1 1.1 reshape.506
  15.2 3.6 %all-to-all-start = ((bf16[2,2,65536]{2,1,0:T(2,128)(2,1)}), bf16[2,2,65536]{2,1,0:T(2,128)(2,1)S(1)}, u32[]{:S(2)}, u32[]{:S(2)}) async-start(bf16[2,2,65536]{2,1,0:T(2,128)(2,1)} %reshape.506), calls=%async_computation | async-start | bytes 1048576 | tf_op jit(solution)/shard_map/all_to_all | solution.py:168
  19.4 9.0 %all-to-all-done = bf16[2,2,65536]{2,1,0:T(2,128)(2,1)S(1)} async-done(((bf16[2,2,65536]{2,1,0:T(2,128)(2,1)}), bf16[2,2,65536]{2,1,0:T(2,128)(2,1)S(1)}, u32[]{:S(2)}, u32[]{:S(2)}) %all-to-all-start) | async-done | bytes 524320 | tf_op jit(solution)/shard_map/all_to_all | solution.py:168
  28.4 0.5 reshape.507
  29.4 209.3 %all-gather.2.cloned.1.call-done = bf16[128,64,1024]{2,1,0:T(8,128)(2,1)} async-done(((bf16[1,64,1024]{2,1,0:T(8,128)(2,1)}), bf16[128,64,1024]{2,1,0:T(8,128)(2,1)}) %all-gather.2.cloned.1.call-update) | async-done | bytes 16777232 | tf_op jit(solution)/shard_map/all_gather | solution.py:32
  238.8 8.9 %reduce_sum.30 = bf16[64,1024]{1,0:T(8,128)(2,1)S(1)} reduce(bf16[128,64,1024]{2,1,0:T(8,128)(2,1)} %all-gather.2.cloned.1.call-done, bf16[]{:T(256)} %constant.592.clone.1), dimensions={0}, to_apply=%region_0.1 | reduce | flops 8323072 | bytes 16908290 | tf_op jit(solution)/shard_map/reduce_sum | solution.py:32
  248.2 6.4 %pmax.7 = f32[64]{0:T(128)S(1)} all-reduce(f32[64]{0:T(128)S(1)} %get-tuple-element.460), channel_id=1, replica_groups=mesh['pair'=128,'trow'=2] {'trow'}, use_global_device_ids=true, to_apply=%region_5.6 | all-reduce | flops 64 | bytes 512 | tf_op jit(solution)/shard_map/pmax | solution.py:135
  254.8 4.6 %collective-permute-start = (bf16[1,64,32]{2,1,0:T(8,128)(2,1)S(1)}, bf16[1,64,32]{2,1,0:T(8,128)(2,1)S(1)}, u32[]{:S(2)}, u32[]{:S(2)}) collective-permute-start(bf16[1,64,32]{2,1,0:T(8,128)(2,1)S(1)} %get-tuple-element.565), channel_id=1, source_target_pairs={{0,1},{2,3},{4,5},{6,7},{8,9},{10,11},{12,13},{14,15},{16,17},{18,... | collective-permute-start | bytes 12296 | tf_op jit(solution)/shard_map/ppermute | solution.py:21
  259.4 1.3 collective-permute-start.1
  260.8 5.7 %collective-permute-done.1 = bf16[1,64,32]{2,1,0:T(8,128)(2,1)S(1)} collective-permute-done((bf16[1,64,32]{2,1,0:T(8,128)(2,1)S(1)}, bf16[1,64,32]{2,1,0:T(8,128)(2,1)S(1)}, u32[]{:S(2)}, u32[]{:S(2)}) %collective-permute-start.1) | collective-permute-done | bytes 4128 | tf_op jit(solution)/shard_map/ppermute | solution.py:23
  266.7 10.5 %while.45 = (s32[]{:T(128)}, f32[2,16,64,128]{3,1,2,0:T(8,128)S(1)}, s32[2]{0:T(128)S(1)}, bf16[1,64,320]{2,1,0:T(8,128)(2,1)S(1)}, bf16[144,9]{0,1:T(8,128)(2,1...) while((s32[]{:T(128)}, f32[2,16,64,128]{3,1,2,0:T(8,128)S(1)}, s32[2]{0:T(128)S(1)}, ...), condition=%wide.region_7.8_spmd, body=%wide.region_6.7_spmd.sunk | while | flops 23512260 | bytes 14720639 | solution.py:104
  266.7 0.7 dynamic_slice.71
  269.1 0.5 concatenate.223
  269.6 0.8 convolution_bitcast_fusion.6
  270.7 1.2 fusion.97
  272.0 0.7 dynamic_slice.71
  274.4 0.5 concatenate.223
  274.8 0.8 convolution_bitcast_fusion.6
  275.9 1.2 fusion.97
  277.5 1.7 collective-permute-start.2
  279.2 1.5 collective-permute-start.3
  281.1 1.9 collective-permute-done.2
  283.0 5.9 %collective-permute-done.3 = bf16[16,64,32]{2,0,1:T(8,128)(2,1)S(1)} collective-permute-done((bf16[16,64,32]{2,0,1:T(8,128)(2,1)S(1)}, bf16[16,64,32]{2,0,1:T(8,128)(2,1)S(1)}, u32[]{:S(2)}, u32[]{:S(2)}) %collective-permute-start.3) | collective-permute-done | bytes 65568 | tf_op jit(solution)/shard_map/ppermute | solution.py:23
  288.9 0.5 pad_maximum_fusion
  289.5 11.9 %while.46 = (s32[]{:T(128)}, f32[2,16,64,128]{3,1,2,0:T(8,128)S(1)}, s32[2]{0:T(128)S(1)}, bf16[16,64,320]{2,0,1:T(8,128)(2,1)S(1)}, bf16[144,144]{1,0:T(8,128)(...) while((s32[]{:T(128)}, f32[2,16,64,128]{3,1,2,0:T(8,128)S(1)}, s32[2]{0:T(128)S(1)}, ...), condition=%wide.region_9.10_spmd, body=%wide.region_8.9_spmd.sunk | while | flops 342569024 | bytes 24628092 | solution.py:104
  289.5 0.7 dynamic_slice.73
  290.8 0.4 constant_dynamic-slice_fusion.9
  293.2 0.8 convolution_bitcast_fusion.7
  294.2 1.2 fusion.104
  295.5 0.7 dynamic_slice.73
  299.1 0.8 convolution_bitcast_fusion.7
  300.2 1.2 fusion.104
  301.8 1.5 collective-permute-start.4
  303.2 1.3 collective-permute-start.5
  305.3 1.8 collective-permute-done.4
  307.1 5.9 %collective-permute-done.5 = bf16[16,64,32]{2,0,1:T(8,128)(2,1)S(1)} collective-permute-done((bf16[16,64,32]{2,0,1:T(8,128)(2,1)S(1)}, bf16[16,64,32]{2,0,1:T(8,128)(2,1)S(1)}, u32[]{:S(2)}, u32[]{:S(2)}) %collective-permute-start.5) | collective-permute-done | bytes 65568 | tf_op jit(solution)/shard_map/ppermute | solution.py:23
  313.0 0.5 pad_maximum_fusion.1
  313.5 11.1 %while.47 = (s32[]{:T(128)}, f32[2,1,64,128]{3,2,1,0:T(8,128)S(1)}, s32[2]{0:T(128)S(1)}, bf16[16,64,320]{2,0,1:T(8,128)(2,1)S(1)}, bf16[9,144]{1,0:T(8,128)(2,1...) while((s32[]{:T(128)}, f32[2,1,64,128]{3,2,1,0:T(8,128)S(1)}, s32[2]{0:T(128)S(1)}, ...), condition=%wide.region_11.12_spmd, body=%wide.region_10.11_spmd.sunk | while | flops 21975112 | bytes 11917275 | solution.py:104
  313.5 0.6 dynamic_slice.75
  314.8 0.4 constant_dynamic-slice_fusion.10
  317.8 1.3 fusion.111
  319.1 0.6 dynamic_slice.75
  323.3 1.3 fusion.111
  324.6 0.6 bitcast_select_fusion
  (181 shorter events, 15.0 us)
Async XLA Ops:
  6.5 232.2 %all-gather.2.cloned.1.call-start = ((), (), s32[]{:S(2)}) async-start(), calls=%async_computation.1 | async-start | bytes 16908288 | tf_op jit(solution)/shard_map/all_gather | solution.py:32
  15.2 13.2 %all-to-all-start = ((bf16[2,2,65536]{2,1,0:T(2,128)(2,1)}), bf16[2,2,65536]{2,1,0:T(2,128)(2,1)S(1)}, u32[]{:S(2)}, u32[]{:S(2)}) async-start(bf16[2,2,65536]{2,1,0:T(2,128)(2,1)} %reshape.506), calls=%async_computation | async-start | bytes 1048576 | tf_op jit(solution)/shard_map/all_to_all | solution.py:168
  29.4 231.2 %copy-start.1 = (bf16[16,1,3,3,3,3]{0,5,4,3,2,1:T(4,128)(2,1)S(1)}, bf16[16,1,3,3,3,3]{0,5,4,3,2,1:T(4,128)(2,1)}, u32[]{:S(2)}) copy-start(bf16[16,1,3,3,3,3]{0,5,4,3,2,1:T(4,128)(2,1)} %param.20) | copy-start | bytes 7780
  254.8 6.0 %collective-permute-start = (bf16[1,64,32]{2,1,0:T(8,128)(2,1)S(1)}, bf16[1,64,32]{2,1,0:T(8,128)(2,1)S(1)}, u32[]{:S(2)}, u32[]{:S(2)}) collective-permute-start(bf16[1,64,32]{2,1,0:T(8,128)(2,1)S(1)} %get-tuple-element.565), channel_id=1, source_target_pairs={{0,1},{2,3},{4,5},{6,7},{8,9},{10,11},{12,13},{14,15},{16,17},{18,... | collective-permute-start | bytes 12296 | tf_op jit(solution)/shard_map/ppermute | solution.py:21
  259.4 7.1 %collective-permute-start.1 = (bf16[1,64,32]{2,1,0:T(8,128)(2,1)S(1)}, bf16[1,64,32]{2,1,0:T(8,128)(2,1)S(1)}, u32[]{:S(2)}, u32[]{:S(2)}) collective-permute-start(bf16[1,64,32]{2,1,0:T(8,128)(2,1)S(1)} %get-tuple-element.566), channel_id=1, source_target_pairs={{1,0},{3,2},{5,4},{7,6},{9,8},{11,10},{13,12},{15,14},{17,16},{19,... | collective-permute-start | bytes 12296 | tf_op jit(solution)/shard_map/ppermute | solution.py:23
  266.7 10.5 %copy-start.3 = (f32[16]{0:T(128)S(1)}, f32[16]{0:T(128)}, u32[]{:S(2)}) copy-start(f32[16]{0:T(128)} %param.21) | copy-start | bytes 196
  277.2 3.5 %copy-start = (bf16[16,16,3,3,3,3]{1,0,5,4,3,2:T(8,128)(2,1)S(1)}, bf16[16,16,3,3,3,3]{1,0,5,4,3,2:T(8,128)(2,1)}, u32[]{:S(2)}) copy-start(bf16[16,16,3,3,3,3]{1,0,5,4,3,2:T(8,128)(2,1)} %param.22) | copy-start | bytes 124420
  277.5 5.5 %collective-permute-start.2 = (bf16[16,64,32]{2,0,1:T(8,128)(2,1)S(1)}, bf16[16,64,32]{2,0,1:T(8,128)(2,1)S(1)}, u32[]{:S(2)}, u32[]{:S(2)}) collective-permute-start(bf16[16,64,32]{2,0,1:T(8,128)(2,1)S(1)} %get-tuple-element.563), channel_id=1, source_target_pairs={{0,1},{2,3},{4,5},{6,7},{8,9},{10,11},{12,13},{14,15},{16,17},{18,... | collective-permute-start | bytes 196616 | tf_op jit(solution)/shard_map/ppermute | solution.py:21
  279.2 9.8 %collective-permute-start.3 = (bf16[16,64,32]{2,0,1:T(8,128)(2,1)S(1)}, bf16[16,64,32]{2,0,1:T(8,128)(2,1)S(1)}, u32[]{:S(2)}, u32[]{:S(2)}) collective-permute-start(bf16[16,64,32]{2,0,1:T(8,128)(2,1)S(1)} %get-tuple-element.564), channel_id=1, source_target_pairs={{1,0},{3,2},{5,4},{7,6},{9,8},{11,10},{13,12},{15,14},{17,16},{19,... | collective-permute-start | bytes 196616 | tf_op jit(solution)/shard_map/ppermute | solution.py:23
  289.5 12.0 %copy-start.4 = (f32[16]{0:T(128)S(1)}, f32[16]{0:T(128)}, u32[]{:S(2)}) copy-start(f32[16]{0:T(128)} %param.23) | copy-start | bytes 196
  301.5 3.1 copy-start.2
  301.8 5.3 %collective-permute-start.4 = (bf16[16,64,32]{2,0,1:T(8,128)(2,1)S(1)}, bf16[16,64,32]{2,0,1:T(8,128)(2,1)S(1)}, u32[]{:S(2)}, u32[]{:S(2)}) collective-permute-start(bf16[16,64,32]{2,0,1:T(8,128)(2,1)S(1)} %get-tuple-element.561), channel_id=1, source_target_pairs={{0,1},{2,3},{4,5},{6,7},{8,9},{10,11},{12,13},{14,15},{16,17},{18,... | collective-permute-start | bytes 196616 | tf_op jit(solution)/shard_map/ppermute | solution.py:21
  303.2 9.8 %collective-permute-start.5 = (bf16[16,64,32]{2,0,1:T(8,128)(2,1)S(1)}, bf16[16,64,32]{2,0,1:T(8,128)(2,1)S(1)}, u32[]{:S(2)}, u32[]{:S(2)}) collective-permute-start(bf16[16,64,32]{2,0,1:T(8,128)(2,1)S(1)} %get-tuple-element.562), channel_id=1, source_target_pairs={{1,0},{3,2},{5,4},{7,6},{9,8},{11,10},{13,12},{15,14},{17,16},{19,... | collective-permute-start | bytes 196616 | tf_op jit(solution)/shard_map/ppermute | solution.py:23
Sparse Core Ops, SparseCore 0:
  9.2 229.5 all-gather.1
